TPU v7x, 32 devices: a whole 2x2x4 slice. The times are simulated.
32 devices in a mesh: grp: 4 (over y, x), tp: 8 (over z, core).
Axes of the slice: x: 2, y: 2, z: 4, core: 2. Of those that a mesh axis runs over, the one named last changes fastest.
Arguments:
- batch_sizes: int32 [4], P('grp'), may hold values from 1 to 16
- seq_lens: int32 [4, 16], P('grp'), may hold values from 1 to 2048
- page_table: int32 [4, 16, 128], P('grp', None, 'tp'), may hold values from 0 to 255, as said below
- queries: bfloat16 [4, 16, 4096], P('grp', None, 'tp'), may hold values from -4 to 14
- kv_pool: bfloat16 [4, 2048, 16, 1024], P('grp', 'tp'), may hold values from -7 to 7
- new_kv: bfloat16 [4, 16, 1024], P('grp'), may hold values from -6 to 6
- out_weight: bfloat16 [4096, 2880], P('tp', 'grp'), may hold values from -0.375 to 0.375
Outputs:
- mixed: float32 [4, 16, 2880], P('grp')
Inputs may be any that keep to these rules, and one draw needn't show every extreme that they name: `batch_sizes`: slots below a group's batch size are live; the others are empty and their outputs are zero. `seq_lens`: entries of empty slots are drawn but unused. `page_table`: for every group g and every t, the entries [g, :, t * 16 to (t + 1) * 16 - 1] are a permutation of 0 to 255.
All inputs are finite; a program needn't handle non-finite values.
Results may differ from a plain program's by a relative error of at most 0.007.
Values may be sent and summed in bfloat16 or wider, within the bound.
A program may use at most 64 MiB of HBM per device.

v0:
```python
import jax
import jax.numpy as jnp
from jax import lax
from jax.sharding import PartitionSpec as P

HEADS = 64
KV_HEADS = 8
HD = 64
SLOT_BLOCK = 2
PRECISE = lax.Precision.HIGHEST
NEG_BIG = -1e30


def attend_slots(query_rows, page_blocks, lengths, tp_index, tp_count, kv_heads):
    slot_count, page_count, page_len, row_width = page_blocks.shape
    head_dim = row_width // (2 * kv_heads)
    head_count = query_rows.shape[1] // head_dim
    group_size = head_count // kv_heads
    token_count = page_count * page_len
    token_rows = page_blocks.reshape(slot_count, token_count, row_width)
    key_rows = token_rows[:, :, : row_width // 2].reshape(
        slot_count, token_count, kv_heads, head_dim
    )
    value_rows = token_rows[:, :, row_width // 2 :].reshape(
        slot_count, token_count, kv_heads, head_dim
    )
    grouped = query_rows.reshape(slot_count, kv_heads, group_size, head_dim)
    scores = jnp.einsum("skgd,stkd->skgt", grouped, key_rows, preferred_element_type=jnp.float32)
    scores = scores * head_dim ** (-0.5)
    page_index = lax.broadcasted_iota(jnp.int32, (page_count, page_len), 0)
    token_index = lax.broadcasted_iota(jnp.int32, (page_count, page_len), 1)
    position = ((page_index * tp_count + tp_index) * page_len + token_index).reshape(token_count)
    valid_mask = (position[None, :] < lengths[:, None])[:, None, None, :]
    scores = jnp.where(valid_mask, scores, NEG_BIG)
    top_score = jnp.max(scores, axis=3)
    weights = jnp.where(valid_mask, jnp.exp(scores - top_score[..., None]), 0.0)
    weight_sum = jnp.sum(weights, axis=3)
    weighted = jnp.einsum(
        "skgt,stkd->skgd",
        weights.astype(jnp.bfloat16),
        value_rows,
        preferred_element_type=jnp.float32,
    )
    return (
        weighted.reshape(slot_count, head_count * head_dim),
        top_score.reshape(slot_count, head_count),
        weight_sum.reshape(slot_count, head_count),
    )


def local(batch_sizes, seq_lens, page_table, queries, kv_pool, new_kv, out_weight):
    tp_count = lax.axis_size("tp")
    tp_index = lax.axis_index("tp")
    gathered = lax.all_gather(queries, "tp", axis=2, tiled=True)[0]
    kv_pages = kv_pool[0]
    page_ids = page_table[0]
    lengths = seq_lens[0]
    live_count = batch_sizes[0]
    slot_count, full_width = gathered.shape
    head_dim = HD
    head_count = HEADS
    slot_order = jnp.arange(slot_count, dtype=jnp.int32)

    def local_block(block_index, state):
        first_slot = block_index * SLOT_BLOCK
        query_rows = lax.dynamic_slice_in_dim(gathered, first_slot, SLOT_BLOCK, 0)
        block_ids = lax.dynamic_slice_in_dim(page_ids, first_slot, SLOT_BLOCK, 0)
        block_lengths = lax.dynamic_slice_in_dim(lengths, first_slot, SLOT_BLOCK, 0)
        block_slots = first_slot + jnp.arange(SLOT_BLOCK, dtype=jnp.int32)
        block_lengths = jnp.where(block_slots < live_count, block_lengths, 0)
        pieces = attend_slots(
            query_rows, kv_pages[block_ids], block_lengths, tp_index, tp_count, KV_HEADS
        )
        return tuple(
            (
                lax.dynamic_update_slice_in_dim(whole, piece, first_slot, 0)
                for whole, piece in zip(state, pieces)
            )
        )

    start_state = (
        jnp.zeros((slot_count, full_width), jnp.float32),
        jnp.full((slot_count, head_count), NEG_BIG, jnp.float32),
        jnp.zeros((slot_count, head_count), jnp.float32),
    )
    block_total = (live_count + SLOT_BLOCK - 1) // SLOT_BLOCK
    weighted, top_score, weight_sum = lax.fori_loop(0, block_total, local_block, start_state)
    own_heads = head_count // tp_count
    own_width = own_heads * head_dim
    shard_weighted, shard_top, shard_sum = (
        lax.all_to_all(weighted[None], "tp", split_axis=2, concat_axis=0, tiled=True),
        lax.all_to_all(top_score[None], "tp", split_axis=2, concat_axis=0, tiled=True),
        lax.all_to_all(weight_sum[None], "tp", split_axis=2, concat_axis=0, tiled=True),
    )
    part_top = jnp.max(shard_top, axis=0)
    shard_rescale = jnp.exp(shard_top - part_top[None])
    part_weighted = jnp.sum(shard_weighted * jnp.repeat(shard_rescale, head_dim, axis=-1), axis=0)
    part_sum = jnp.sum(shard_sum * shard_rescale, axis=0)
    fresh_rows = new_kv[0].astype(jnp.float32)
    kv_width = KV_HEADS * head_dim
    new_keys = fresh_rows[:, :kv_width].reshape(slot_count, KV_HEADS, head_dim)
    new_values = fresh_rows[:, kv_width:].reshape(slot_count, KV_HEADS, head_dim)
    head_ids = tp_index * own_heads + jnp.arange(own_heads, dtype=jnp.int32)
    head_map = (
        head_ids[:, None] // (head_count // KV_HEADS)
        == jnp.arange(KV_HEADS, dtype=jnp.int32)[None, :]
    ).astype(jnp.float32)
    own_keys = jnp.einsum("jk,skd->sjd", head_map, new_keys, precision=PRECISE)
    own_values = jnp.einsum("jk,skd->sjd", head_map, new_values, precision=PRECISE)
    own_queries = queries[0].astype(jnp.float32).reshape(slot_count, own_heads, head_dim)
    self_score = jnp.sum(own_queries * own_keys, axis=-1) * head_dim ** (-0.5)
    final_top = jnp.maximum(part_top, self_score)
    cache_rescale = jnp.exp(part_top - final_top)
    self_rescale = jnp.exp(self_score - final_top)
    numerator = part_weighted.reshape(slot_count, own_heads, head_dim) * cache_rescale[..., None]
    numerator = numerator + own_values * self_rescale[..., None]
    denominator = part_sum * cache_rescale + self_rescale
    attended = (numerator / denominator[..., None]).reshape(slot_count, own_width)
    attended = jnp.where((slot_order < live_count)[:, None], attended, 0.0).astype(jnp.bfloat16)
    projected = jnp.dot(
        attended,
        lax.all_gather(out_weight, "grp", axis=1, tiled=True),
        preferred_element_type=jnp.float32,
    )
    mixed = lax.psum(projected, "tp")
    return mixed[None]


def solution(mesh):
    return jax.shard_map(
        local,
        mesh=mesh,
        in_specs=(
            P("grp"),
            P("grp", None),
            P("grp", None, "tp"),
            P("grp", None, "tp"),
            P("grp", "tp", None, None),
            P("grp", None, None),
            P("tp", "grp"),
        ),
        out_specs=P("grp", None, None),
        check_vma=False,
    )
```

profile of v0, /device:TPU:0, one launch (start us, length us, event | category | flops | bytes accessed | tf_op | source)
XLA Modules:
  0.0 214.4 jit_solution(14500293375372935720)
XLA Ops:
  6.5 0.7 all-gather.2.cloned.1.call-update
  7.9 15.9 %all_gather.6 = bf16[1,16,4096]{2,1,0:T(8,128)(2,1)S(1)} all-gather(bf16[1,16,512]{2,1,0:T(8,128)(2,1)} %param.12), channel_id=1, replica_groups=mesh['grp'=4,'tp'=8] {'tp'}, dimensions={2}, use_global_device_ids=true | all-gather | bytes 147456 | tf_op jit(solution)/shard_map/all_gather | solution.py:54
  23.9 65.7 %while.14 = (s32[]{:T(128)}, f32[16,4096]{1,0:T(8,128)S(1)}, f32[16,64]{1,0:T(8,128)S(1)}, f32[16,64]{1,0:T(8,128)S(1)}, s32[]{:T(128)}, /*index=5*/s32[]{:T(128...) while((s32[]{:T(128)}, f32[16,4096]{1,0:T(8,128)S(1)}, ...), condition=%wide.region_3.4_spmd, body=%wide.region_0.3_spmd.sunk | while | flops 8685212 | bytes 7998579 | solution.py:87
  24.0 1.4 compare_select_fusion.8
  26.4 4.0 %gather_fusion = bf16[32,16,1024]{2,1,0:T(8,128)(2,1)S(1)} fusion(bf16[256,16,1024]{2,1,0:T(8,128)(2,1)} %get-tuple-element.223, s32[1024]{0:T(1024)S(1)} %pad_clamp_fusion.2), kind=kCustom, calls=%fused_computation.clone.1 | custom fusion | bytes 2097280 | tf_op jit(solution)/shard_map/while/body/gather | solution.py:72
  32.1 1.4 compare_select_fusion.8
  34.5 4.5 %gather_fusion = bf16[32,16,1024]{2,1,0:T(8,128)(2,1)S(1)} fusion(bf16[256,16,1024]{2,1,0:T(8,128)(2,1)} %get-tuple-element.223, s32[1024]{0:T(1024)S(1)} %pad_clamp_fusion.2), kind=kCustom, calls=%fused_computation.clone.1 | custom fusion | bytes 2097280 | tf_op jit(solution)/shard_map/while/body/gather | solution.py:72
  40.8 1.4 compare_select_fusion.8
  43.2 4.0 %gather_fusion = bf16[32,16,1024]{2,1,0:T(8,128)(2,1)S(1)} fusion(bf16[256,16,1024]{2,1,0:T(8,128)(2,1)} %get-tuple-element.223, s32[1024]{0:T(1024)S(1)} %pad_clamp_fusion.2), kind=kCustom, calls=%fused_computation.clone.1 | custom fusion | bytes 2097280 | tf_op jit(solution)/shard_map/while/body/gather | solution.py:72
  48.9 1.4 compare_select_fusion.8
  51.3 4.0 %gather_fusion = bf16[32,16,1024]{2,1,0:T(8,128)(2,1)S(1)} fusion(bf16[256,16,1024]{2,1,0:T(8,128)(2,1)} %get-tuple-element.223, s32[1024]{0:T(1024)S(1)} %pad_clamp_fusion.2), kind=kCustom, calls=%fused_computation.clone.1 | custom fusion | bytes 2097280 | tf_op jit(solution)/shard_map/while/body/gather | solution.py:72
  57.0 1.4 compare_select_fusion.8
  59.5 4.0 %gather_fusion = bf16[32,16,1024]{2,1,0:T(8,128)(2,1)S(1)} fusion(bf16[256,16,1024]{2,1,0:T(8,128)(2,1)} %get-tuple-element.223, s32[1024]{0:T(1024)S(1)} %pad_clamp_fusion.2), kind=kCustom, calls=%fused_computation.clone.1 | custom fusion | bytes 2097280 | tf_op jit(solution)/shard_map/while/body/gather | solution.py:72
  65.2 1.4 compare_select_fusion.8
  67.6 4.0 %gather_fusion = bf16[32,16,1024]{2,1,0:T(8,128)(2,1)S(1)} fusion(bf16[256,16,1024]{2,1,0:T(8,128)(2,1)} %get-tuple-element.223, s32[1024]{0:T(1024)S(1)} %pad_clamp_fusion.2), kind=kCustom, calls=%fused_computation.clone.1 | custom fusion | bytes 2097280 | tf_op jit(solution)/shard_map/while/body/gather | solution.py:72
  73.3 1.4 compare_select_fusion.8
  75.7 4.0 %gather_fusion = bf16[32,16,1024]{2,1,0:T(8,128)(2,1)S(1)} fusion(bf16[256,16,1024]{2,1,0:T(8,128)(2,1)} %get-tuple-element.223, s32[1024]{0:T(1024)S(1)} %pad_clamp_fusion.2), kind=kCustom, calls=%fused_computation.clone.1 | custom fusion | bytes 2097280 | tf_op jit(solution)/shard_map/while/body/gather | solution.py:72
  81.5 1.4 compare_select_fusion.8
  83.9 4.0 %gather_fusion = bf16[32,16,1024]{2,1,0:T(8,128)(2,1)S(1)} fusion(bf16[256,16,1024]{2,1,0:T(8,128)(2,1)} %get-tuple-element.223, s32[1024]{0:T(1024)S(1)} %pad_clamp_fusion.2), kind=kCustom, calls=%fused_computation.clone.1 | custom fusion | bytes 2097280 | tf_op jit(solution)/shard_map/while/body/gather | solution.py:72
  91.6 4.6 %all-to-all-start.1 = ((f32[8,1,128]{2,1,0:T(1,128)}), f32[8,1,128]{2,1,0:T(1,128)S(1)}, u32[]{:S(2)}, u32[]{:S(2)}) async-start(f32[8,1,128]{2,1,0:T(1,128)} %reshape.169), calls=%async_computation.1 | async-start | bytes 8192 | tf_op jit(solution)/shard_map/all_to_all | solution.py:92
  96.4 0.7 reduce.3
  97.9 3.9 %all-to-all-done.1 = f32[8,1,128]{2,1,0:T(1,128)S(1)} async-done(((f32[8,1,128]{2,1,0:T(1,128)}), f32[8,1,128]{2,1,0:T(1,128)S(1)}, u32[]{:S(2)}, u32[]{:S(2)}) %all-to-all-start.1) | async-done | bytes 4128 | tf_op jit(solution)/shard_map/all_to_all | solution.py:92
  101.8 3.3 %all-to-all-start.2 = ((f32[8,1,128]{2,1,0:T(1,128)}), f32[8,1,128]{2,1,0:T(1,128)S(1)}, u32[]{:S(2)}, u32[]{:S(2)}) async-start(f32[8,1,128]{2,1,0:T(1,128)} %reshape.171), calls=%async_computation.2 | async-start | bytes 8192 | tf_op jit(solution)/shard_map/all_to_all | solution.py:93
  106.0 19.3 %reduce.1 = f32[4096,16]{1,0:T(8,128)} reduce(f32[4096,1,16]{2,1,0:T(1,128)S(1)} %bitcast.84, f32[]{:T(128)} %broadcast.132), dimensions={1}, to_apply=%bitcast.54.reduce_sub_computation | reduce | bytes 524292
  125.3 3.0 %reshape.167 = f32[8,1,8192]{2,1,0:T(1,128)} reshape(f32[4096,16]{1,0:T(8,128)} %reduce.1) | data formatting | bytes 524288
  128.3 5.0 %all-to-all-start = ((f32[8,1,8192]{2,1,0:T(1,128)}), f32[8,1,8192]{2,1,0:T(1,128)S(1)}, u32[]{:S(2)}, u32[]{:S(2)}) async-start(f32[8,1,8192]{2,1,0:T(1,128)} %reshape.167), calls=%async_computation | async-start | bytes 524288 | tf_op jit(solution)/shard_map/all_to_all | solution.py:91
  135.5 7.5 %all-to-all-done = f32[8,1,8192]{2,1,0:T(1,128)S(1)} async-done(((f32[8,1,8192]{2,1,0:T(1,128)}), f32[8,1,8192]{2,1,0:T(1,128)S(1)}, u32[]{:S(2)}, u32[]{:S(2)}) %all-to-all-start) | async-done | bytes 262176 | tf_op jit(solution)/shard_map/all_to_all | solution.py:91
  143.1 1.2 reduce.2
  144.3 3.9 %reshape.168 = f32[4096,1,16]{2,1,0:T(1,128)S(1)} reshape(f32[8,8192]{1,0:T(8,128)S(1)} %reduce.2) | data formatting | bytes 524288
  149.0 3.4 %convolution_bitcast_fusion = f32[1,16,2880]{2,1,0:T(8,128)} fusion(bf16[512,2880]{0,1:T(8,128)(2,1)} %all-gather.2.cloned.1.call-done, bf16[16,512]{1,0:T(8,128)(2,1)S(1)} %reshape.153, pred[16]{0:T(512)(128)(4,1)S(1)} %iota_compare_fusion.1), kind=kOutput, calls=%fused_computation.22 | convolution fusion | flops 47194112 | bytes 3149840 | tf_op jit(solution)/shard_map/dot_general | solution.py:120
  152.4 53.6 %all-reduce.2.cloned.1.call-done = f32[1,16,2880]{2,1,0:T(8,128)} async-done(((f32[1,16,2880]{2,1,0:T(8,128)}), f32[1,16,2880]{2,1,0:T(8,128)}) %all-reduce.2.cloned.1.call-update) | async-done | bytes 184336 | tf_op jit(solution)/shard_map/psum | solution.py:125
  206.0 1.6 copy.58
  (201 shorter events, 28.2 us)
Async XLA Ops:
  6.5 142.4 %all-gather.2.cloned.1.call-start = ((), (), s32[]{:S(2)}) async-start(), calls=%async_computation.3 | async-start | bytes 3686400 | tf_op jit(solution)/shard_map/all_gather | solution.py:122
  23.9 72.3 %copy-start.1 = (bf16[1,16,1024]{2,1,0:T(8,128)(2,1)S(1)}, bf16[1,16,1024]{2,1,0:T(8,128)(2,1)}, u32[]{:S(2)}) copy-start(bf16[1,16,1024]{2,1,0:T(8,128)(2,1)} %param.14) | copy-start | bytes 98308
  23.9 72.3 %copy-start = (bf16[1,16,512]{2,1,0:T(8,128)(2,1)S(1)}, bf16[1,16,512]{2,1,0:T(8,128)(2,1)}, u32[]{:S(2)}) copy-start(bf16[1,16,512]{2,1,0:T(8,128)(2,1)} %param.12) | copy-start | bytes 49156
  91.6 10.2 %all-to-all-start.1 = ((f32[8,1,128]{2,1,0:T(1,128)}), f32[8,1,128]{2,1,0:T(1,128)S(1)}, u32[]{:S(2)}, u32[]{:S(2)}) async-start(f32[8,1,128]{2,1,0:T(1,128)} %reshape.169), calls=%async_computation.1 | async-start | bytes 8192 | tf_op jit(solution)/shard_map/all_to_all | solution.py:92
  101.8 26.5 %all-to-all-start.2 = ((f32[8,1,128]{2,1,0:T(1,128)}), f32[8,1,128]{2,1,0:T(1,128)S(1)}, u32[]{:S(2)}, u32[]{:S(2)}) async-start(f32[8,1,128]{2,1,0:T(1,128)} %reshape.171), calls=%async_computation.2 | async-start | bytes 8192 | tf_op jit(solution)/shard_map/all_to_all | solution.py:93
  128.3 14.7 %all-to-all-start = ((f32[8,1,8192]{2,1,0:T(1,128)}), f32[8,1,8192]{2,1,0:T(1,128)S(1)}, u32[]{:S(2)}, u32[]{:S(2)}) async-start(f32[8,1,8192]{2,1,0:T(1,128)} %reshape.167), calls=%async_computation | async-start | bytes 524288 | tf_op jit(solution)/shard_map/all_to_all | solution.py:91
  133.4 72.6 %all-reduce.2.cloned.1.call-start = ((), (), s32[]{:S(2)}) async-start(), calls=%async_computation.4 | async-start | bytes 376832 | tf_op jit(solution)/shard_map/psum | solution.py:125
Sparse Core Ops, SparseCore 0:
  9.2 44.9 all-gather.1
  152.5 53.4 all-reduce.1
where the time goes:
time: 216 us; the launch traced here: 214 us
  waiting for transfers between devices  65.8 us (30%)
  local copies, waits for them, and re-layouts  53.4 us (25%)
  other arithmetic  42.9 us (20%)
  blocking collectives  15.9 us (7%)
  between operations  14.3 us (7%)
  starting transfers between devices  13.2 us (6%)
  matrix products  8.29 us (4%)
    psum x1, waiting for transfers between devices, local(): mixed = lax.psum(projected, 'tp')  53.6 us
    gather x8, local copies, waits for them, and re-layouts, local_block(): kv_pages[block_ids]  32.4 us
    unnamed x3, other arithmetic  20.7 us
    all_gather x1, blocking collectives, local(): gathered = lax.all_gather(queries, 'tp', axis=2, tiled=True)[0]  15.9 us
    select_n x8, other arithmetic, local_block(): block_lengths = jnp.where(block_slots < live_count, block_lengths, 0)  11 us
    unnamed x12, local copies, waits for them, and re-layouts  10.6 us
    all_to_all x1, waiting for transfers between devices, local(): lax.all_to_all(weighted[None], 'tp', split_axis=2, concat_axis=0, tiled=T...  7.53 us
    select_n x8, other arithmetic, local_block(): kv_pages[block_ids]  5.57 us
  transfers between devices with their start and end apart: 5, of which 3 were waited for; matrix products, arithmetic and copies ran while one was open for 46% of the time, Pallas kernels for 0%

commit v1 on v0

--- a/solution.py
+++ b/solution.py
@@ -9,6 +9,14 @@
 SLOT_BLOCK = 2
 PRECISE = lax.Precision.HIGHEST
 NEG_BIG = -1e30
+
+
+def added_up(shard, axis):
+    count, total = (lax.axis_size(axis), shard)
+    for hop in [1 << k for k in range(count.bit_length() - 1)]:
+        swap = [(i, i ^ hop) for i in range(count)]
+        total = total + lax.ppermute(total, axis, swap)
+    return total
 
 
 def attend_slots(query_rows, page_blocks, lengths, tp_index, tp_count, kv_heads):
@@ -122,7 +130,7 @@
         lax.all_gather(out_weight, "grp", axis=1, tiled=True),
         preferred_element_type=jnp.float32,
     )
-    mixed = lax.psum(projected, "tp")
+    mixed = added_up(projected, "tp")
     return mixed[None]
 
 

time: 216 us -> 180 us (0.83)
  waiting for transfers between devices: 65.8 us -> 31.2 us
    psum x1 -> x0, waiting for transfers between devices: 53.6 us -> none  [local(): mixed = lax.psum(projected, 'tp')]
    ppermute x0 -> x3, waiting for transfers between devices: none -> 18.8 us  [added_up(): total = total + lax.ppermute(total, axis, swap)]
    unnamed x12 -> x11, local copies, waits for them, and re-layouts: 10.6 us -> 9.02 us
  transfers between devices with their start and end apart: 5 -> 7, of which waited for: 3 -> 5; matrix products, arithmetic and copies ran while one was open for 46% -> 56% of each run, Pallas kernels for 0% -> 0%
where the time goes in v1:
time: 180 us; the launch traced here: 178 us
  local copies, waits for them, and re-layouts  51.8 us (29%)
  other arithmetic  43.6 us (24%)
  waiting for transfers between devices  31.2 us (17%)
  blocking collectives  15.9 us (9%)
  between operations  14.3 us (8%)
  starting transfers between devices  13.3 us (7%)
  matrix products  7.59 us (4%)
    gather x8, local copies, waits for them, and re-layouts, local_block(): kv_pages[block_ids]  32.4 us
    unnamed x3, other arithmetic  20.7 us
    ppermute x3, waiting for transfers between devices, added_up(): total = total + lax.ppermute(total, axis, swap)  18.8 us
    all_gather x1, blocking collectives, local(): gathered = lax.all_gather(queries, 'tp', axis=2, tiled=True)[0]  15.9 us
    select_n x8, other arithmetic, local_block(): block_lengths = jnp.where(block_slots < live_count, block_lengths, 0)  11 us
    unnamed x11, local copies, waits for them, and re-layouts  9.02 us
    all_to_all x1, waiting for transfers between devices, local(): lax.all_to_all(weighted[None], 'tp', split_axis=2, concat_axis=0, tiled=T...  7.76 us
    select_n x8, other arithmetic, local_block(): kv_pages[block_ids]  5.57 us
  transfers between devices with their start and end apart: 7, of which 5 were waited for; matrix products, arithmetic and copies ran while one was open for 56% of the time, Pallas kernels for 0%

profile of v1, /device:TPU:0, one launch (start us, length us, event | category | flops | bytes accessed | tf_op | source)
XLA Modules:
  0.0 178.4 jit_solution(17001580891018461481)
XLA Ops:
  6.5 0.7 all-gather.2.cloned.1.call-update
  7.9 15.9 %all_gather.6 = bf16[1,16,4096]{2,1,0:T(8,128)(2,1)S(1)} all-gather(bf16[1,16,512]{2,1,0:T(8,128)(2,1)} %param.12), channel_id=1, replica_groups=mesh['grp'=4,'tp'=8] {'tp'}, dimensions={2}, use_global_device_ids=true | all-gather | bytes 147456 | tf_op jit(solution)/shard_map/all_gather | solution.py:62
  23.9 65.7 %while.14 = (s32[]{:T(128)}, f32[16,4096]{1,0:T(8,128)S(1)}, f32[16,64]{1,0:T(8,128)S(1)}, f32[16,64]{1,0:T(8,128)S(1)}, s32[]{:T(128)}, /*index=5*/s32[]{:T(128...) while((s32[]{:T(128)}, f32[16,4096]{1,0:T(8,128)S(1)}, ...), condition=%wide.region_3.4_spmd, body=%wide.region_0.3_spmd.sunk | while | flops 8685212 | bytes 7998579 | solution.py:95
  24.0 1.4 compare_select_fusion.8
  26.4 4.0 %gather_fusion = bf16[32,16,1024]{2,1,0:T(8,128)(2,1)S(1)} fusion(bf16[256,16,1024]{2,1,0:T(8,128)(2,1)} %get-tuple-element.223, s32[1024]{0:T(1024)S(1)} %pad_clamp_fusion.2), kind=kCustom, calls=%fused_computation.clone.1 | custom fusion | bytes 2097280 | tf_op jit(solution)/shard_map/while/body/gather | solution.py:80
  32.1 1.4 compare_select_fusion.8
  34.5 4.5 %gather_fusion = bf16[32,16,1024]{2,1,0:T(8,128)(2,1)S(1)} fusion(bf16[256,16,1024]{2,1,0:T(8,128)(2,1)} %get-tuple-element.223, s32[1024]{0:T(1024)S(1)} %pad_clamp_fusion.2), kind=kCustom, calls=%fused_computation.clone.1 | custom fusion | bytes 2097280 | tf_op jit(solution)/shard_map/while/body/gather | solution.py:80
  40.7 1.4 compare_select_fusion.8
  43.2 4.0 %gather_fusion = bf16[32,16,1024]{2,1,0:T(8,128)(2,1)S(1)} fusion(bf16[256,16,1024]{2,1,0:T(8,128)(2,1)} %get-tuple-element.223, s32[1024]{0:T(1024)S(1)} %pad_clamp_fusion.2), kind=kCustom, calls=%fused_computation.clone.1 | custom fusion | bytes 2097280 | tf_op jit(solution)/shard_map/while/body/gather | solution.py:80
  48.9 1.4 compare_select_fusion.8
  51.3 4.0 %gather_fusion = bf16[32,16,1024]{2,1,0:T(8,128)(2,1)S(1)} fusion(bf16[256,16,1024]{2,1,0:T(8,128)(2,1)} %get-tuple-element.223, s32[1024]{0:T(1024)S(1)} %pad_clamp_fusion.2), kind=kCustom, calls=%fused_computation.clone.1 | custom fusion | bytes 2097280 | tf_op jit(solution)/shard_map/while/body/gather | solution.py:80
  57.0 1.4 compare_select_fusion.8
  59.4 4.0 %gather_fusion = bf16[32,16,1024]{2,1,0:T(8,128)(2,1)S(1)} fusion(bf16[256,16,1024]{2,1,0:T(8,128)(2,1)} %get-tuple-element.223, s32[1024]{0:T(1024)S(1)} %pad_clamp_fusion.2), kind=kCustom, calls=%fused_computation.clone.1 | custom fusion | bytes 2097280 | tf_op jit(solution)/shard_map/while/body/gather | solution.py:80
  65.2 1.4 compare_select_fusion.8
  67.6 4.0 %gather_fusion = bf16[32,16,1024]{2,1,0:T(8,128)(2,1)S(1)} fusion(bf16[256,16,1024]{2,1,0:T(8,128)(2,1)} %get-tuple-element.223, s32[1024]{0:T(1024)S(1)} %pad_clamp_fusion.2), kind=kCustom, calls=%fused_computation.clone.1 | custom fusion | bytes 2097280 | tf_op jit(solution)/shard_map/while/body/gather | solution.py:80
  73.3 1.4 compare_select_fusion.8
  75.7 4.0 %gather_fusion = bf16[32,16,1024]{2,1,0:T(8,128)(2,1)S(1)} fusion(bf16[256,16,1024]{2,1,0:T(8,128)(2,1)} %get-tuple-element.223, s32[1024]{0:T(1024)S(1)} %pad_clamp_fusion.2), kind=kCustom, calls=%fused_computation.clone.1 | custom fusion | bytes 2097280 | tf_op jit(solution)/shard_map/while/body/gather | solution.py:80
  81.5 1.4 compare_select_fusion.8
  83.9 4.0 %gather_fusion = bf16[32,16,1024]{2,1,0:T(8,128)(2,1)S(1)} fusion(bf16[256,16,1024]{2,1,0:T(8,128)(2,1)} %get-tuple-element.223, s32[1024]{0:T(1024)S(1)} %pad_clamp_fusion.2), kind=kCustom, calls=%fused_computation.clone.1 | custom fusion | bytes 2097280 | tf_op jit(solution)/shard_map/while/body/gather | solution.py:80
  91.6 4.6 %all-to-all-start.1 = ((f32[8,1,128]{2,1,0:T(1,128)}), f32[8,1,128]{2,1,0:T(1,128)S(1)}, u32[]{:S(2)}, u32[]{:S(2)}) async-start(f32[8,1,128]{2,1,0:T(1,128)} %reshape.169), calls=%async_computation.1 | async-start | bytes 8192 | tf_op jit(solution)/shard_map/all_to_all | solution.py:100
  97.9 3.9 %all-to-all-done.1 = f32[8,1,128]{2,1,0:T(1,128)S(1)} async-done(((f32[8,1,128]{2,1,0:T(1,128)}), f32[8,1,128]{2,1,0:T(1,128)S(1)}, u32[]{:S(2)}, u32[]{:S(2)}) %all-to-all-start.1) | async-done | bytes 4128 | tf_op jit(solution)/shard_map/all_to_all | solution.py:100
  101.8 3.3 %all-to-all-start.2 = ((f32[8,1,128]{2,1,0:T(1,128)}), f32[8,1,128]{2,1,0:T(1,128)S(1)}, u32[]{:S(2)}, u32[]{:S(2)}) async-start(f32[8,1,128]{2,1,0:T(1,128)} %reshape.171), calls=%async_computation.2 | async-start | bytes 8192 | tf_op jit(solution)/shard_map/all_to_all | solution.py:101
  106.0 19.3 %reduce.1 = f32[4096,16]{1,0:T(8,128)} reduce(f32[4096,1,16]{2,1,0:T(1,128)S(1)} %bitcast.84, f32[]{:T(128)} %broadcast.132), dimensions={1}, to_apply=%bitcast.54.reduce_sub_computation | reduce | bytes 524292
  125.3 3.0 %reshape.167 = f32[8,1,8192]{2,1,0:T(1,128)} reshape(f32[4096,16]{1,0:T(8,128)} %reduce.1) | data formatting | bytes 524288
  128.3 5.0 %all-to-all-start = ((f32[8,1,8192]{2,1,0:T(1,128)}), f32[8,1,8192]{2,1,0:T(1,128)S(1)}, u32[]{:S(2)}, u32[]{:S(2)}) async-start(f32[8,1,8192]{2,1,0:T(1,128)} %reshape.167), calls=%async_computation | async-start | bytes 524288 | tf_op jit(solution)/shard_map/all_to_all | solution.py:99
  135.3 7.8 %all-to-all-done = f32[8,1,8192]{2,1,0:T(1,128)S(1)} async-done(((f32[8,1,8192]{2,1,0:T(1,128)}), f32[8,1,8192]{2,1,0:T(1,128)S(1)}, u32[]{:S(2)}, u32[]{:S(2)}) %all-to-all-start) | async-done | bytes 262176 | tf_op jit(solution)/shard_map/all_to_all | solution.py:99
  143.1 1.2 reduce.2
  144.3 3.9 %reshape.168 = f32[4096,1,16]{2,1,0:T(1,128)S(1)} reshape(f32[8,8192]{1,0:T(8,128)S(1)} %reduce.2) | data formatting | bytes 524288
  148.9 2.7 %fusion.15 = f32[16,2880]{1,0:T(8,128)S(1)} fusion(bf16[512,2880]{0,1:T(8,128)(2,1)} %all-gather.2.cloned.1.call-done, bf16[16,512]{1,0:T(8,128)(2,1)S(1)} %reshape.153, pred[16]{0:T(512)(128)(4,1)S(1)} %iota_compare_fusion.1), kind=kOutput, calls=%fused_computation.35 | convolution fusion | flops 47194112 | bytes 3149840 | tf_op jit(solution)/shard_map/dot_general | solution.py:128
  151.7 1.4 collective-permute-done
  153.3 6.7 %collective-permute-done.1 = f32[16,2880]{1,0:T(8,128)S(1)} collective-permute-done((f32[16,2880]{1,0:T(8,128)S(1)}, f32[16,2880]{1,0:T(8,128)S(1)}, u32[]{:S(2)}, u32[]{:S(2)}) %collective-permute-start.1) | collective-permute-done | bytes 184352 | tf_op jit(solution)/shard_map/ppermute | solution.py:18
  160.2 10.7 %collective-permute-done.2 = f32[16,2880]{1,0:T(8,128)S(1)} collective-permute-done((f32[16,2880]{1,0:T(8,128)S(1)}, f32[16,2880]{1,0:T(8,128)S(1)}, u32[]{:S(2)}, u32[]{:S(2)}) %collective-permute-start.2) | collective-permute-done | bytes 184352 | tf_op jit(solution)/shard_map/ppermute | solution.py:18
  (206 shorter events, 29.7 us)
Async XLA Ops:
  6.5 142.4 %all-gather.2.cloned.1.call-start = ((), (), s32[]{:S(2)}) async-start(), calls=%async_computation.3 | async-start | bytes 3686400 | tf_op jit(solution)/shard_map/all_gather | solution.py:130
  23.9 72.3 %copy-start.1 = (bf16[1,16,1024]{2,1,0:T(8,128)(2,1)S(1)}, bf16[1,16,1024]{2,1,0:T(8,128)(2,1)}, u32[]{:S(2)}) copy-start(bf16[1,16,1024]{2,1,0:T(8,128)(2,1)} %param.14) | copy-start | bytes 98308
  23.9 72.3 %copy-start = (bf16[1,16,512]{2,1,0:T(8,128)(2,1)S(1)}, bf16[1,16,512]{2,1,0:T(8,128)(2,1)}, u32[]{:S(2)}) copy-start(bf16[1,16,512]{2,1,0:T(8,128)(2,1)} %param.12) | copy-start | bytes 49156
  91.6 10.2 %all-to-all-start.1 = ((f32[8,1,128]{2,1,0:T(1,128)}), f32[8,1,128]{2,1,0:T(1,128)S(1)}, u32[]{:S(2)}, u32[]{:S(2)}) async-start(f32[8,1,128]{2,1,0:T(1,128)} %reshape.169), calls=%async_computation.1 | async-start | bytes 8192 | tf_op jit(solution)/shard_map/all_to_all | solution.py:100
  101.8 26.5 %all-to-all-start.2 = ((f32[8,1,128]{2,1,0:T(1,128)}), f32[8,1,128]{2,1,0:T(1,128)S(1)}, u32[]{:S(2)}, u32[]{:S(2)}) async-start(f32[8,1,128]{2,1,0:T(1,128)} %reshape.171), calls=%async_computation.2 | async-start | bytes 8192 | tf_op jit(solution)/shard_map/all_to_all | solution.py:101
  128.3 14.7 %all-to-all-start = ((f32[8,1,8192]{2,1,0:T(1,128)}), f32[8,1,8192]{2,1,0:T(1,128)S(1)}, u32[]{:S(2)}, u32[]{:S(2)}) async-start(f32[8,1,8192]{2,1,0:T(1,128)} %reshape.167), calls=%async_computation | async-start | bytes 524288 | tf_op jit(solution)/shard_map/all_to_all | solution.py:99
  151.6 1.5 collective-permute-start
  153.1 6.8 %collective-permute-start.1 = (f32[16,2880]{1,0:T(8,128)S(1)}, f32[16,2880]{1,0:T(8,128)S(1)}, u32[]{:S(2)}, u32[]{:S(2)}) collective-permute-start(f32[16,2880]{1,0:T(8,128)S(1)} %add.86), channel_id=1, source_target_pairs={{0,2},{1,3},{2,0},{3,1},{4,6},{5,7},{6,4},{7,5},{8,10},{9,11},{10,... | collective-permute-start | bytes 552968 | tf_op jit(solution)/shard_map/ppermute | solution.py:18
  160.0 10.9 %collective-permute-start.2 = (f32[16,2880]{1,0:T(8,128)S(1)}, f32[16,2880]{1,0:T(8,128)S(1)}, u32[]{:S(2)}, u32[]{:S(2)}) collective-permute-start(f32[16,2880]{1,0:T(8,128)S(1)} %add.87), channel_id=1, source_target_pairs={{0,4},{1,5},{2,6},{3,7},{4,0},{5,1},{6,2},{7,3},{8,12},{9,13},{10,... | collective-permute-start | bytes 552968 | tf_op jit(solution)/shard_map/ppermute | solution.py:18
Sparse Core Ops, SparseCore 0:
  9.2 44.9 all-gather.1
